TPU v7x, 32 devices: a whole 2x2x4 slice. The times are simulated.
32 devices in a mesh: amp: 4 (over y, core), own: 8 (over z, x).
Axes of the slice: x: 2, y: 2, z: 4, core: 2. Of those that a mesh axis runs over, the one named last changes fastest.
Arguments:
- amplitudes: bfloat16 [32, 2304, 192], P('own', None, 'amp'), may hold values from -6 to 6
- integrals: bfloat16 [32, 1152, 2304], P('own'), as said below
- occ_irrep: int32 [34], replicated, may hold values from 0 to 7, as said below
- tile_irrep: int32 [18], replicated, may hold values from 0 to 7, as said below
Outputs:
- cycle_term: bfloat16 [2304, 2304], P(('amp', 'own'))
Inputs may be any that keep to these rules, and one draw needn't show every extreme that they name: `occ_irrep`: labels of the D2h group, combined by XOR; every label occurs, and all labels occur equally often up to one. `tile_irrep`: labels of the D2h group, combined by XOR; every label occurs, and all labels occur equally often up to one, so some label has exactly 3 tiles. integrals[k, c, (j, b)] is zero unless the labels of k, c, j and b combine by XOR to 0.
All inputs are finite; a program needn't handle non-finite values.
Results may differ from a plain program's by a relative error of at most 0.001.
Values may be sent and summed in bfloat16 or wider, within the bound.
A program may use at most 128 MiB of HBM per device.

v0:
```python
import jax
import jax.numpy as jnp
from jax import lax
from jax.sharding import PartitionSpec as P

V = 1152
TILE = 64
NI = 2


def tile_ranks(tile_irrep):
    count = tile_irrep.shape[0]
    index = jnp.arange(count, dtype=jnp.int32)
    same = (tile_irrep[:, None] == tile_irrep[None, :]) & (index[None, :] < index[:, None])
    return jnp.sum(same.astype(jnp.int32), axis=1)


def shards(amplitudes, integrals, occ_irrep, tile_irrep):
    amp_index = lax.axis_index("amp")
    own_index = lax.axis_index("own")
    n_amp = lax.axis_size("amp")
    n_own = lax.axis_size("own")
    regrouped = lax.all_to_all(amplitudes, "amp", split_axis=1, concat_axis=2, tiled=True)
    k_local, rows, packed_width = regrouped.shape
    slot_count = packed_width // TILE
    virt_lab = jnp.repeat(tile_irrep, TILE)
    row_all = jnp.bitwise_xor(jnp.repeat(occ_irrep[:NI], V), jnp.tile(virt_lab, NI))
    row_lab = lax.dynamic_slice_in_dim(row_all, amp_index * rows, rows)
    k_lab = lax.dynamic_slice_in_dim(occ_irrep, NI + own_index * k_local, k_local)
    wanted = jnp.bitwise_xor(k_lab[:, None], row_lab[None, :])
    ranks = tile_ranks(tile_irrep)
    slot_ids = jnp.arange(slot_count, dtype=jnp.int32)
    select = (tile_irrep[None, None, None, :] == wanted[:, :, None, None]) & (
        ranks[None, None, None, :] == slot_ids[None, None, :, None]
    )
    pieces = regrouped.reshape(k_local, rows, slot_count, TILE)
    dense = jnp.einsum(
        "krjt,krje->krte", select.astype(jnp.bfloat16), pieces, preferred_element_type=jnp.float32
    )
    masked = dense.reshape(k_local, rows, V).astype(jnp.bfloat16)
    summed = lax.psum_scatter(
        jnp.einsum("kmc,kcn->mn", masked, integrals, preferred_element_type=jnp.float32),
        "own",
        scatter_dimension=0,
        tiled=True,
    )
    share = summed.shape[0]
    blocks = summed.reshape(share, n_amp, n_own, share)
    moved = lax.all_to_all(
        lax.all_to_all(blocks, "amp", split_axis=1, concat_axis=1, tiled=True),
        "own",
        split_axis=2,
        concat_axis=2,
        tiled=True,
    )
    mirrored = jnp.transpose(moved, (3, 1, 2, 0)).reshape(share, NI * V)
    return (summed + mirrored).astype(jnp.bfloat16)


def solution(mesh):
    return jax.shard_map(
        shards,
        mesh=mesh,
        in_specs=(P("own", None, "amp"), P("own", None, None), P(), P()),
        out_specs=P(("amp", "own"), None),
        check_vma=False,
    )
```

profile of v0, /device:TPU:0, one launch (start us, length us, event | category | flops | bytes accessed | tf_op | source)
XLA Modules:
  0.0 252.3 jit_solution(9332235532349839505)
XLA Ops:
  6.5 3.6 %copy.25 = bf16[4,2304,48]{2,0,1:T(4,128)(2,1)S(1)} copy(bf16[4,2304,48]{1,2,0:T(8,128)(2,1)} %param.4) | data formatting | bytes 1769472 | tf_op args[0]
  10.1 0.0 copy-start.1
  10.1 0.0 copy-start.2
  10.1 4.6 %reshape.80 = bf16[4,2,55296]{2,1,0:T(2,128)(2,1)} reshape(bf16[2304,4,48]{2,1,0:T(4,128)(2,1)S(1)} %bitcast.18) | data formatting | bytes 1769472
  14.8 4.2 %all-to-all-start = ((bf16[4,2,55296]{2,1,0:T(2,128)(2,1)}), bf16[4,2,55296]{2,1,0:T(2,128)(2,1)S(1)}, u32[]{:S(2)}, u32[]{:S(2)}) async-start(bf16[4,2,55296]{2,1,0:T(2,128)(2,1)} %reshape.80), calls=%async_computation | async-start | bytes 1769472 | tf_op jit(solution)/shard_map/all_to_all | solution.py:23
  19.0 0.0 reduce-scatter.2.cloned.1.call-start
  19.0 0.0 copy-done.1
  19.0 0.2 convert_reduce_fusion
  19.2 0.1 broadcast_in_dim.5
  19.3 0.1 tile.8
  19.3 0.0 copy-done.2
  19.3 0.1 dynamic_slice.6
  19.4 0.1 broadcast_xor_fusion.1
  19.5 0.1 dynamic_slice.7
  19.6 0.1 broadcast_xor_fusion
  19.7 1.1 broadcast_compare_fusion
  20.8 10.9 %all-to-all-done = bf16[4,2,55296]{2,1,0:T(2,128)(2,1)S(1)} async-done(((bf16[4,2,55296]{2,1,0:T(2,128)(2,1)}), bf16[4,2,55296]{2,1,0:T(2,128)(2,1)S(1)}, u32[]{:S(2)}, u32[]{:S(2)}) %all-to-all-start) | async-done | bytes 884768 | tf_op jit(solution)/shard_map/all_to_all | solution.py:23
  31.7 2.4 reshape.81
  34.1 1.5 copy.27
  35.6 1.5 copy.28
  37.1 11.1 %convolution_convert_fusion = bf16[4,576,18,64]{3,2,1,0:T(8,128)(2,1)} fusion(bf16[4,576,3,64]{3,2,1,0:T(4,128)(2,1)S(1)} %copy.28, pred[3,18]{1,0:T(4,128)(4,1)S(1)} %iota_compare_fusion.1, pred[4,576,18]{2,1,0:T(8,128)(4,1)} %broadcast_compare_fusion), kind=kOutput, calls=%fused_computation | convolution fusion | flops 18703872 | bytes 6234678 | tf_op jit(solution)/shard_map/krjt,krje->krte/dot_general | solution.py:37
  48.2 15.5 %copy.29 = bf16[4,576,18,64]{1,3,2,0:T(8,128)(2,1)} copy(bf16[4,576,18,64]{3,2,1,0:T(8,128)(2,1)} %convolution_convert_fusion) | data formatting | bytes 10616832 | tf_op jit(solution)/shard_map/convert_element_type | solution.py:40
  63.7 19.2 %convolution_bitcast_fusion = f32[576,2304]{1,0:T(8,128)} fusion(bf16[4,576,1152]{1,2,0:T(8,128)(2,1)} %bitcast.19, bf16[4,1152,2304]{2,1,0:T(8,128)(2,1)} %param.5), kind=kOutput, calls=%fused_computation.1 | convolution fusion | flops 12230590464 | bytes 31850496 | tf_op jit(solution)/shard_map/kmc,kcn->mn/dot_general | solution.py:42
  82.8 0.0 reduce-scatter.2.cloned.1.call-update
  82.9 105.3 %reduce-scatter.2.cloned.1.call-done = f32[72,2304]{1,0:T(8,128)} async-done(((f32[576,2304]{1,0:T(8,128)}), f32[72,2304]{1,0:T(8,128)}) %reduce-scatter.2.cloned.1.call-update) | async-done | bytes 663568 | tf_op jit(solution)/shard_map/reduce_scatter | solution.py:41
  188.2 2.3 reshape.77
  190.5 0.9 copy.31
  191.4 18.4 %all_to_all.25 = f32[72,4,8,72]{0,2,3,1:T(8,128)S(1)} all-to-all(f32[72,4,8,72]{0,2,3,1:T(8,128)S(1)} %copy.31), channel_id=1, replica_groups=mesh['amp'=4,'own'=8] {'amp'}, dimensions={1} | all-to-all | bytes 1327104 | tf_op jit(solution)/shard_map/all_to_all | solution.py:50
  209.8 0.8 copy.32
  210.6 32.7 %all_to_all.26 = f32[72,4,8,72]{0,1,3,2:T(4,128)S(1)} all-to-all(f32[72,4,8,72]{0,1,3,2:T(4,128)S(1)} %copy.32), channel_id=1, replica_groups=mesh['amp'=4,'own'=8] {'own'}, dimensions={2} | all-to-all | bytes 1327104 | tf_op jit(solution)/shard_map/all_to_all | solution.py:49
  243.3 0.0 copy-start
  243.3 0.7 copy.33
  244.0 0.6 reshape.78
  244.7 0.0 copy-done
  244.7 0.8 add_convert_fusion
  (2 shorter events, 0.0 us)
Async XLA Ops:
  10.1 8.9 %copy-start.1 = (s32[18]{0:T(128)S(1)}, s32[18]{0:T(128)}, u32[]{:S(2)}) copy-start(s32[18]{0:T(128)} %param.7) | copy-start | bytes 220
  10.1 9.2 %copy-start.2 = (s32[34]{0:T(128)S(1)}, s32[34]{0:T(128)}, u32[]{:S(2)}) copy-start(s32[34]{0:T(128)} %param.6) | copy-start | bytes 412
  14.8 16.9 %all-to-all-start = ((bf16[4,2,55296]{2,1,0:T(2,128)(2,1)}), bf16[4,2,55296]{2,1,0:T(2,128)(2,1)S(1)}, u32[]{:S(2)}, u32[]{:S(2)}) async-start(bf16[4,2,55296]{2,1,0:T(2,128)(2,1)} %reshape.80), calls=%async_computation | async-start | bytes 1769472 | tf_op jit(solution)/shard_map/all_to_all | solution.py:23
  19.0 169.2 %reduce-scatter.2.cloned.1.call-start = ((), (), s32[]{:S(2)}) async-start(), calls=%async_computation.4 | async-start | bytes 5971968 | tf_op jit(solution)/shard_map/reduce_scatter | solution.py:41
  243.3 1.3 copy-start
Sparse Core Ops, SparseCore 0:
  83.0 105.1 reduce-scatter.1
where the time goes:
time: 253 us; the launch traced here: 252 us
  waiting for transfers between devices  116 us (46%)
  blocking collectives  51.1 us (20%)
  local copies, waits for them, and re-layouts  34.7 us (14%)
  matrix products  30.3 us (12%)
  between operations  13.5 us (5%)
  starting transfers between devices  4.24 us (2%)
    reduce_scatter x1, waiting for transfers between devices, shards(): lax.psum_scatter(jnp.einsum('kmc,kcn->mn', masked, integrals, preferred_e...  105 us
    all_to_all x1, blocking collectives, shards(): lax.all_to_all(lax.all_to_all(blocks, 'amp', split_axis=1, concat_axis=1,...  32.7 us
    dot_general x1, matrix products, shards(): jnp.einsum('kmc,kcn->mn', masked, integrals, preferred_element_type=jnp.f...  19.2 us
    all_to_all x1, blocking collectives, shards(): lax.all_to_all(blocks, 'amp', split_axis=1, concat_axis=1, tiled=True)  18.4 us
    convert_element_type x1, local copies, waits for them, and re-layouts, shards(): masked = dense.reshape(k_local, rows, V).astype(jnp.bfloat16)  15.5 us
    dot_general x1, matrix products, shards(): jnp.einsum('krjt,krje->krte', select.astype(jnp.bfloat16), pieces, prefer...  11.1 us
    all_to_all x1, waiting for transfers between devices, shards(): lax.all_to_all(amplitudes, 'amp', split_axis=1, concat_axis=2, tiled=True)  10.9 us
    unnamed x9, local copies, waits for them, and re-layouts  10.6 us
  transfers between devices with their start and end apart: 2, of which 2 were waited for; matrix products, arithmetic and copies ran while one was open for 1% of the time, Pallas kernels for 0%

commit v1 on v0

v1 whole, which is shorter than its diff:
```python
import functools

import jax
import jax.numpy as jnp
from jax import lax
from jax.experimental import pallas as pl
from jax.experimental.pallas import tpu as pltpu
from jax.sharding import PartitionSpec as P

TILE = 64
NI = 2
LABELS = 8
LANES = 128
MESH = pl.DeviceIdType.MESH


def gcd(a, b):
    return a if b == 0 else gcd(b, a % b)


def half_of(block, odd):
    return jnp.where(odd, block[:, TILE:], block[:, :TILE])


def local_kernel(n_tiles, slots, amp_ref, int_ref, occ_ref, tile_ref, out_ref, meta_ref, w_ref, tile_of, row_of, count, sems):
    k_local, rows, width = amp_ref.shape
    pieces, grain = w_ref.shape[1], w_ref.shape[2]
    wide = NI * slots
    amp_index = lax.axis_index("amp")
    own_index = lax.axis_index("own")

    for i in range(LABELS):
        count[i] = 0
        for s in range(slots):
            tile_of[i * slots + s] = -1
        for q in range(wide):
            row_of[i * wide + q] = -1
    for t in range(n_tiles):
        lab = tile_ref[t]
        rank = count[lab]
        tile_of[lab * slots + rank] = t
        count[lab] = rank + 1

    def copy_of(k, lab, j):
        at = amp_index * width + j * grain
        t = tile_of[lab * slots + at // TILE]
        start = pl.multiple_of(jnp.maximum(t, 0) * TILE + at % TILE, grain)
        copy = pltpu.make_async_copy(
            int_ref.at[k, pl.ds(start, grain), :], w_ref.at[k * LABELS + lab, j], sems.at[k, lab, j]
        )
        return t, copy

    for k in range(k_local):
        for lab in range(LABELS):
            for j in range(pieces):
                t, copy = copy_of(k, lab, j)

                @pl.when(t >= 0)
                def _():
                    copy.start()

                @pl.when(t < 0)
                def _():
                    w_ref[k * LABELS + lab, j] = jnp.zeros((grain, rows), w_ref.dtype)

    for i in range(LABELS):
        count[i] = 0
    for u in range(NI * n_tiles):
        lab = jnp.bitwise_xor(occ_ref[u // n_tiles], tile_ref[u % n_tiles])
        rank = count[lab]
        row_of[lab * wide + rank] = u
        count[lab] = rank + 1
        meta_ref[u] = lab
        meta_ref[NI * n_tiles + u] = rank

    k_lab = [occ_ref[NI + own_index * k_local + k] for k in range(k_local)]

    for k in range(k_local):
        for lab in range(LABELS):
            for j in range(pieces):
                t, copy = copy_of(k, lab, j)

                @pl.when(t >= 0)
                def _():
                    copy.wait()

    def block(lab, carry):
        tiles = [jnp.maximum(row_of[lab * wide + q], 0) for q in range(wide)]
        a = jnp.concatenate(
            [
                jnp.concatenate(
                    [amp_ref[k, pl.ds(pl.multiple_of(u * TILE, TILE), TILE), :] for k in range(k_local)], axis=1
                )
                for u in tiles
            ],
            axis=0,
        )
        stack = []
        for k in range(k_local):
            at = k * LABELS + jnp.bitwise_xor(lab, k_lab[k])
            halves = []
            for u in tiles:
                lanes = pl.ds(pl.multiple_of(u // 2 * LANES, LANES), LANES)
                x = w_ref[at, :, :, lanes].reshape(pieces * grain, LANES)
                halves.append(half_of(x, u % 2 == 1))
            stack.append(jnp.concatenate(halves, axis=1))
        w = jnp.concatenate(stack, axis=0)
        p = jnp.dot(a, w, preferred_element_type=jnp.float32)
        s = p + p.T
        for q in range(wide):
            u = row_of[lab * wide + q]

            @pl.when(u >= 0)
            def _():
                for c in range(out_ref.shape[0]):
                    out_ref[c, pl.ds(pl.multiple_of(u * TILE, TILE), TILE), :] = s[
                        q * TILE : (q + 1) * TILE, c * LANES : (c + 1) * LANES
                    ]

        return carry

    lax.fori_loop(0, LABELS, block, 0)


def orders(amp_bits, own_bits):
    core = [("amp", 0)]
    y = [("amp", b) for b in range(1, amp_bits)]
    near = [("own", 0)]
    far = [("own", b) for b in range(1, own_bits)]
    return [core + y + near + far, core + near + y + far, core + far + y + near]


def bit_of(name, bit):
    return lax.axis_index(name) // 2**bit % 2


def partner_of(name, bit):
    return {name: lax.axis_index(name) + (1 - 2 * bit_of(name, bit)) * 2**bit}


def scatter_kernel(plans, x_ref, out_ref, *scratch):
    stages = len(plans[0])
    accs = [[scratch[(c * stages + s) * 2] for s in range(stages)] for c in range(len(plans))]
    recvs = [[scratch[(c * stages + s) * 2 + 1] for s in range(stages)] for c in range(len(plans))]
    send_sems, recv_sems = scratch[-2:]

    barrier = pltpu.get_barrier_semaphore()
    for name, bit, _ in plans[0]:
        pl.semaphore_signal(barrier, inc=1, device_id=partner_of(name, bit), device_id_type=MESH)
    pl.semaphore_wait(barrier, stages)

    def copy_of(c, s):
        name, bit, axis = plans[c][s]
        held = x_ref.at[c] if s == 0 else accs[c][s - 1]
        return pltpu.make_async_remote_copy(
            src_ref=held.at[(slice(None),) * axis + (1 - bit_of(name, bit),)],
            dst_ref=recvs[c][s],
            send_sem=send_sems.at[c, s],
            recv_sem=recv_sems.at[c, s],
            device_id=partner_of(name, bit),
            device_id_type=MESH,
        )

    for c in range(len(plans)):
        copy_of(c, 0).start()
    for s in range(stages):
        for c in range(len(plans)):
            name, bit, axis = plans[c][s]
            copy_of(c, s).wait_recv()
            held = x_ref.at[c] if s == 0 else accs[c][s - 1]
            index = (slice(None),) * axis + (bit_of(name, bit),)
            total = held[index] + recvs[c][s][...]
            if s + 1 < stages:
                accs[c][s][...] = total
                copy_of(c, s + 1).start()
            else:
                out_ref[c] = total
    for s in range(stages):
        for c in range(len(plans)):
            copy_of(c, s).wait_send()


def expand_kernel(n_tiles, x_ref, meta_ref, out_ref):
    chunks, share, _ = x_ref.shape
    count = NI * n_tiles
    base = (lax.axis_index("amp") * lax.axis_size("own") + lax.axis_index("own")) * share
    first = base // TILE
    row = base + lax.broadcasted_iota(jnp.int32, (share, LANES), 0)
    lane = lax.broadcasted_iota(jnp.int32, (share, LANES), 1)
    row_lab = jnp.where(row < (first + 1) * TILE, meta_ref[first], meta_ref[jnp.minimum(first + 1, count - 1)])
    for pair in range(count // 2):
        labs = [meta_ref[2 * pair + h] for h in range(2)]
        ranks = [meta_ref[count + 2 * pair + h] for h in range(2)]
        halves = [half_of(x_ref[rank // 2], rank % 2 == 1) for rank in ranks]
        col_lab = jnp.where(lane < TILE, labs[0], labs[1])
        dense = jnp.where(row_lab == col_lab, jnp.concatenate(halves, axis=1), 0.0)
        out_ref[:, pair * LANES : (pair + 1) * LANES] = dense.astype(out_ref.dtype)


def shards(amplitudes, integrals, occ_irrep, tile_irrep):
    n_amp = lax.axis_size("amp")
    n_own = lax.axis_size("own")
    k_local, rows, width = amplitudes.shape
    n_tiles = tile_irrep.shape[0]
    slots = width * n_amp // TILE
    grain = gcd(width, TILE)
    chunks = NI * slots * TILE // LANES
    vmem, smem, hbm = (pl.BlockSpec(memory_space=m) for m in (pltpu.VMEM, pltpu.SMEM, pl.ANY))
    packed, meta = pl.pallas_call(
        functools.partial(local_kernel, n_tiles, slots),
        out_shape=(
            jax.ShapeDtypeStruct((chunks, rows, LANES), jnp.float32),
            jax.ShapeDtypeStruct((2 * NI * n_tiles,), jnp.int32),
        ),
        in_specs=[vmem, hbm, smem, smem],
        out_specs=(vmem, smem),
        scratch_shapes=[
            pltpu.VMEM((k_local * LABELS, width // grain, grain, rows), jnp.bfloat16),
            pltpu.SMEM((LABELS * slots,), jnp.int32),
            pltpu.SMEM((LABELS * NI * slots,), jnp.int32),
            pltpu.SMEM((LABELS,), jnp.int32),
            pltpu.SemaphoreType.DMA((k_local, LABELS, width // grain)),
        ],
        compiler_params=pltpu.CompilerParams(vmem_limit_bytes=40 * 2**20),
        name="local",
    )(amplitudes, integrals, occ_irrep, tile_irrep)

    amp_bits, own_bits = n_amp.bit_length() - 1, n_own.bit_length() - 1
    share = rows // (n_amp * n_own)
    plans, scratch = [], []
    for order in orders(amp_bits, own_bits):
        left = [("amp", b) for b in reversed(range(amp_bits))] + [("own", b) for b in reversed(range(own_bits))]
        plan = []
        for name, bit in order:
            axis = left.index((name, bit))
            left.pop(axis)
            plan.append((name, bit, axis))
            scratch += [pltpu.VMEM((2,) * len(left) + (share, LANES), jnp.float32)] * 2
        plans.append(plan)
    stages = amp_bits + own_bits
    summed = pl.pallas_call(
        functools.partial(scatter_kernel, plans),
        out_shape=jax.ShapeDtypeStruct((chunks, share, LANES), jnp.float32),
        in_specs=[vmem],
        out_specs=vmem,
        scratch_shapes=scratch
        + [pltpu.SemaphoreType.DMA((chunks, stages)), pltpu.SemaphoreType.DMA((chunks, stages))],
        compiler_params=pltpu.CompilerParams(
            collective_id=0, has_side_effects=True, vmem_limit_bytes=40 * 2**20
        ),
        name="scatter",
    )(packed.reshape((chunks,) + (2,) * stages + (share, LANES)))

    return pl.pallas_call(
        functools.partial(expand_kernel, n_tiles),
        out_shape=jax.ShapeDtypeStruct((share, rows), jnp.bfloat16),
        in_specs=[vmem, smem],
        out_specs=vmem,
        name="expand",
    )(summed, meta)


def solution(mesh):
    return jax.shard_map(
        shards,
        mesh=mesh,
        in_specs=(P("own", None, "amp"), P("own", None, None), P(), P()),
        out_specs=P(("amp", "own"), None),
        check_vma=False,
    )
```

time: 253 us -> 51.5 us (0.20)
  waiting for transfers between devices: 116 us -> 0 us
  blocking collectives: 51.1 us -> 0 us
  Pallas kernels: 0 us -> 46 us
  matrix products: 30.3 us -> 0 us
  local copies, waits for them, and re-layouts: 34.7 us -> 5.2 us
  between operations: 13.5 us -> 0.05 us
  starting transfers between devices: 4.24 us -> 0 us
    reduce_scatter x1 -> x0, waiting for transfers between devices: 105 us -> none  [shards(): lax.psum_scatter(jnp.einsum('kmc,kcn->mn', masked, integrals, preferred_e...]
    all_to_all x2 -> x0, blocking collectives: 51.1 us -> none  [the longest x1 32.7 us: shards(): lax.all_to_all(lax.all_to_all(blocks, 'amp', split_axis=1, concat_axis=1,...]
    pallas_call x0 -> x3, Pallas kernels: none -> 46 us  [the longest x1 31.5 us: shards(): pl.pallas_call(functools.partial(scatter_kernel, plans), out_shape=jax.Sh...]
    dot_general x2 -> x0, matrix products: 30.3 us -> none  [the longest x1 19.2 us: shards(): jnp.einsum('kmc,kcn->mn', masked, integrals, preferred_element_type=jnp.f...]
    convert_element_type x1 -> x0, local copies, waits for them, and re-layouts: 15.5 us -> none  [shards(): masked = dense.reshape(k_local, rows, V).astype(jnp.bfloat16)]
    all_to_all x1 -> x0, waiting for transfers between devices: 10.9 us -> none  [shards(): lax.all_to_all(amplitudes, 'amp', split_axis=1, concat_axis=2, tiled=True)]
    unnamed x9, local copies, waits for them, and re-layouts: 10.6 us -> 5.2 us
    reshape x4 -> x0, local copies, waits for them, and re-layouts: 5.37 us -> none  [the longest x2 3.23 us: shards(): blocks = summed.reshape(share, n_amp, n_own, share)]
  transfers between devices with their start and end apart: 2 -> 0, of which waited for: 2 -> 0; matrix products, arithmetic and copies ran while one was open for 1% -> 0% of each run, Pallas kernels for 0% -> 0%
where the time goes in v1:
time: 51.5 us; the launch traced here: 51.2 us
  Pallas kernels  46 us (89%)
  local copies, waits for them, and re-layouts  5.2 us (10%)
    pallas_call x1, Pallas kernels, shards(): pl.pallas_call(functools.partial(scatter_kernel, plans), out_shape=jax.Sh...  31.5 us
    pallas_call x1, Pallas kernels, shards(): pl.pallas_call(functools.partial(local_kernel, n_tiles, slots), out_shape...  11.7 us
    unnamed x9, local copies, waits for them, and re-layouts  5.2 us
    pallas_call x1, Pallas kernels, shards(): pl.pallas_call(functools.partial(expand_kernel, n_tiles), out_shape=jax.S...  2.79 us

profile of v1, /device:TPU:0, one launch (start us, length us, event | category | flops | bytes accessed | tf_op | source)
XLA Modules:
  0.0 51.2 jit_solution(12168840912750528937)
XLA Ops:
  0.0 2.7 %copy.5.amp_ref = bf16[4,2304,48]{2,1,0:T(8,128)(2,1)S(1)} copy(bf16[4,2304,48]{1,2,0:T(8,128)(2,1)} %param.4) | data formatting | bytes 1769472 | tf_op args[0]
  2.7 0.0 copy-start.1
  2.7 0.6 %copy-done.1 = s32[34]{0:T(128)S(1)} copy-done((s32[34]{0:T(128)S(1)}, s32[34]{0:T(128)}, u32[]{:S(2)}) %copy-start.1) | copy-done | bytes 160
  3.4 0.0 copy-start.2
  3.4 0.7 %copy-done.2 = s32[18]{0:T(128)S(1)} copy-done((s32[18]{0:T(128)S(1)}, s32[18]{0:T(128)}, u32[]{:S(2)}) %copy-start.2) | copy-done | bytes 96
  4.0 11.7 %local.1 = (f32[3,2304,128]{2,1,0:T(8,128)S(1)}, s32[72]{0:T(128)S(1)}) custom-call(bf16[4,2304,48]{2,1,0:T(8,128)(2,1)S(1)} %copy.5.amp_ref, bf16[4,1152,2304]{2,1,0:T(8,128)(2,1)} %int_ref.1, s32[34]{0:T(128)S(1)} %copy-done.1, s32[18]{0:T(128)S(1)} %copy-done.2), custom_call_target="tpu_custom_call" | custom-call | tf_op jit(solution)/shard_map/local/pallas_call | solution.py:209
  15.7 0.0 copy-start.3
  15.8 0.6 %copy-done.3 = s32[72]{0:T(128)} copy-done((s32[72]{0:T(128)}, s32[72]{0:T(128)S(1)}, u32[]{:S(2)}) %copy-start.3) | copy-done | bytes 312
  16.3 31.5 %scatter.1.x_ref = f32[3,72,128]{2,1,0:T(8,128)S(1)} custom-call(f32[3,2,2,2,2,2,72,128]{7,6,5,4,3,2,1,0:T(8,128)S(1)} %bitcast.1), custom_call_target="tpu_custom_call" | custom-call | tf_op jit(solution)/shard_map/scatter/pallas_call | solution.py:241
  47.8 0.0 copy-start
  47.8 0.6 %copy-done = f32[3,72,128]{2,1,0:T(8,128)} copy-done((f32[3,72,128]{2,1,0:T(8,128)}, f32[3,72,128]{2,1,0:T(8,128)S(1)}, u32[]{:S(2)}) %copy-start) | copy-done | bytes 110616
  48.4 2.8 %expand.1 = bf16[72,2304]{1,0:T(8,128)(2,1)} custom-call(f32[3,72,128]{2,1,0:T(8,128)} %copy-done, s32[72]{0:T(128)} %copy-done.3), custom_call_target="tpu_custom_call" | custom-call | tf_op jit(solution)/shard_map/expand/pallas_call | solution.py:254
Async XLA Ops:
  2.7 0.7 %copy-start.1 = (s32[34]{0:T(128)S(1)}, s32[34]{0:T(128)}, u32[]{:S(2)}) copy-start(s32[34]{0:T(128)} %occ_ref.1) | copy-start | bytes 412
  3.4 0.7 %copy-start.2 = (s32[18]{0:T(128)S(1)}, s32[18]{0:T(128)}, u32[]{:S(2)}) copy-start(s32[18]{0:T(128)} %tile_ref.1) | copy-start | bytes 220
  15.7 0.6 %copy-start.3 = (s32[72]{0:T(128)}, s32[72]{0:T(128)S(1)}, u32[]{:S(2)}) copy-start(s32[72]{0:T(128)S(1)} %get-tuple-element.8.meta_ref) | copy-start | bytes 868
  47.8 0.6 %copy-start = (f32[3,72,128]{2,1,0:T(8,128)}, f32[3,72,128]{2,1,0:T(8,128)S(1)}, u32[]{:S(2)}) copy-start(f32[3,72,128]{2,1,0:T(8,128)S(1)} %scatter.1.x_ref) | copy-start | bytes 331780

commit v2 on v1

--- a/solution.py
+++ b/solution.py
@@ -1,4 +1,5 @@
 import functools
+import itertools
 
 import jax
 import jax.numpy as jnp
@@ -11,6 +12,8 @@
 NI = 2
 LABELS = 8
 LANES = 128
+LEVELS = 32767.0
+LEAST = 1e-30
 MESH = pl.DeviceIdType.MESH
 
 
@@ -22,9 +25,9 @@
     return jnp.where(odd, block[:, TILE:], block[:, :TILE])
 
 
-def local_kernel(n_tiles, slots, amp_ref, int_ref, occ_ref, tile_ref, out_ref, meta_ref, w_ref, tile_of, row_of, count, sems):
-    k_local, rows, width = amp_ref.shape
-    pieces, grain = w_ref.shape[1], w_ref.shape[2]
+def local_kernel(n_tiles, slots, amp_hbm, int_ref, occ_ref, tile_ref, out_ref, meta_ref, amp_ref, w_ref, tile_of, row_of, count, amp_sem, sems):
+    k_local, rows, width = amp_hbm.shape
+    pieces, grain = w_ref.shape[2], w_ref.shape[3]
     wide = NI * slots
     amp_index = lax.axis_index("amp")
     own_index = lax.axis_index("own")
@@ -41,27 +44,27 @@
         tile_of[lab * slots + rank] = t
         count[lab] = rank + 1
 
-    def copy_of(k, lab, j):
+    amp_copy = pltpu.make_async_copy(amp_hbm, amp_ref, amp_sem)
+    amp_copy.start()
+
+    def copy_of(lab, j):
         at = amp_index * width + j * grain
         t = tile_of[lab * slots + at // TILE]
         start = pl.multiple_of(jnp.maximum(t, 0) * TILE + at % TILE, grain)
-        copy = pltpu.make_async_copy(
-            int_ref.at[k, pl.ds(start, grain), :], w_ref.at[k * LABELS + lab, j], sems.at[k, lab, j]
-        )
+        copy = pltpu.make_async_copy(int_ref.at[:, pl.ds(start, grain), :], w_ref.at[lab, :, j], sems.at[lab, j])
         return t, copy
 
-    for k in range(k_local):
-        for lab in range(LABELS):
-            for j in range(pieces):
-                t, copy = copy_of(k, lab, j)
-
-                @pl.when(t >= 0)
-                def _():
-                    copy.start()
-
-                @pl.when(t < 0)
-                def _():
-                    w_ref[k * LABELS + lab, j] = jnp.zeros((grain, rows), w_ref.dtype)
+    for lab in range(LABELS):
+        for j in range(pieces):
+            t, copy = copy_of(lab, j)
+
+            @pl.when(t >= 0)
+            def _():
+                copy.start()
+
+            @pl.when(t < 0)
+            def _():
+                w_ref[lab, :, j] = jnp.zeros((k_local, grain, rows), w_ref.dtype)
 
     for i in range(LABELS):
         count[i] = 0
@@ -75,14 +78,14 @@
 
     k_lab = [occ_ref[NI + own_index * k_local + k] for k in range(k_local)]
 
-    for k in range(k_local):
-        for lab in range(LABELS):
-            for j in range(pieces):
-                t, copy = copy_of(k, lab, j)
-
-                @pl.when(t >= 0)
-                def _():
-                    copy.wait()
+    amp_copy.wait()
+    for lab in range(LABELS):
+        for j in range(pieces):
+            t, copy = copy_of(lab, j)
+
+            @pl.when(t >= 0)
+            def _():
+                copy.wait()
 
     def block(lab, carry):
         tiles = [jnp.maximum(row_of[lab * wide + q], 0) for q in range(wide)]
@@ -97,16 +100,17 @@
         )
         stack = []
         for k in range(k_local):
-            at = k * LABELS + jnp.bitwise_xor(lab, k_lab[k])
+            at = jnp.bitwise_xor(lab, k_lab[k])
             halves = []
             for u in tiles:
                 lanes = pl.ds(pl.multiple_of(u // 2 * LANES, LANES), LANES)
-                x = w_ref[at, :, :, lanes].reshape(pieces * grain, LANES)
+                x = w_ref[at, k, :, :, lanes].reshape(pieces * grain, LANES)
                 halves.append(half_of(x, u % 2 == 1))
             stack.append(jnp.concatenate(halves, axis=1))
         w = jnp.concatenate(stack, axis=0)
-        p = jnp.dot(a, w, preferred_element_type=jnp.float32)
-        s = p + p.T
+        s = jnp.dot(a, w, preferred_element_type=jnp.float32) + lax.dot_general(
+            w, a, (((0,), (1,)), ((), ())), preferred_element_type=jnp.float32
+        )
         for q in range(wide):
             u = row_of[lab * wide + q]
 
@@ -140,44 +144,83 @@
 
 def scatter_kernel(plans, x_ref, out_ref, *scratch):
     stages = len(plans[0])
-    accs = [[scratch[(c * stages + s) * 2] for s in range(stages)] for c in range(len(plans))]
-    recvs = [[scratch[(c * stages + s) * 2 + 1] for s in range(stages)] for c in range(len(plans))]
-    send_sems, recv_sems = scratch[-2:]
+    bufs, at = [], 0
+    for c in range(len(plans)):
+        bufs.append([])
+        for s in range(stages):
+            take = 2 if s == 0 else 5
+            bufs[c].append(scratch[at : at + take])
+            at += take
+    send_sems, recv_sems, scale_send_sems, scale_recv_sems = scratch[at:]
 
     barrier = pltpu.get_barrier_semaphore()
     for name, bit, _ in plans[0]:
         pl.semaphore_signal(barrier, inc=1, device_id=partner_of(name, bit), device_id_type=MESH)
     pl.semaphore_wait(barrier, stages)
 
-    def copy_of(c, s):
-        name, bit, axis = plans[c][s]
-        held = x_ref.at[c] if s == 0 else accs[c][s - 1]
+    def remote(c, s, src, dst, send, recv):
+        name, bit, _ = plans[c][s]
         return pltpu.make_async_remote_copy(
-            src_ref=held.at[(slice(None),) * axis + (1 - bit_of(name, bit),)],
-            dst_ref=recvs[c][s],
-            send_sem=send_sems.at[c, s],
-            recv_sem=recv_sems.at[c, s],
+            src_ref=src,
+            dst_ref=dst,
+            send_sem=send.at[c, s],
+            recv_sem=recv.at[c, s],
             device_id=partner_of(name, bit),
             device_id_type=MESH,
         )
 
+    def copies_of(c, s):
+        name, bit, axis = plans[c][s]
+        if s == 0:
+            src = x_ref.at[(c,) + (slice(None),) * axis + (1 - bit_of(name, bit),)]
+            return [remote(c, s, src, bufs[c][s][1], send_sems, recv_sems)]
+        _, q_send, q_recv, scale_send, scale_recv = bufs[c][s]
+        return [
+            remote(c, s, scale_send, scale_recv, scale_send_sems, scale_recv_sems),
+            remote(c, s, q_send, q_recv, send_sems, recv_sems),
+        ]
+
+    def blocks(count):
+        return itertools.product(range(2), repeat=count)
+
+    def quantize(c, s):
+        name, bit, axis = plans[c][s]
+        _, q_send, _, scale_send, _ = bufs[c][s]
+        away = 1 - bit_of(name, bit)
+        for index in blocks(stages - 1 - s):
+            x = bufs[c][s - 1][0][index[:axis] + (away,) + index[axis:]]
+            most = jnp.maximum(jnp.max(jnp.abs(x), axis=0, keepdims=True), LEAST)
+            q_send[index] = jnp.round(x * (LEVELS / most)).astype(jnp.int32).astype(jnp.int16)
+            scale_send[index] = most * (1.0 / LEVELS)
+
     for c in range(len(plans)):
-        copy_of(c, 0).start()
+        for copy in copies_of(c, 0):
+            copy.start()
     for s in range(stages):
         for c in range(len(plans)):
             name, bit, axis = plans[c][s]
-            copy_of(c, s).wait_recv()
-            held = x_ref.at[c] if s == 0 else accs[c][s - 1]
-            index = (slice(None),) * axis + (bit_of(name, bit),)
-            total = held[index] + recvs[c][s][...]
+            keep = bit_of(name, bit)
+            for copy in copies_of(c, s):
+                copy.wait_recv()
+            for index in blocks(stages - 1 - s):
+                kept = index[:axis] + (keep,) + index[axis:]
+                if s == 0:
+                    total = x_ref[(c,) + kept] + bufs[c][s][1][index]
+                else:
+                    _, _, q_recv, _, scale_recv = bufs[c][s]
+                    total = bufs[c][s - 1][0][kept] + q_recv[index].astype(jnp.int32).astype(jnp.float32) * scale_recv[index]
+                if s + 1 < stages:
+                    bufs[c][s][0][index] = total
+                else:
+                    out_ref[c] = total
             if s + 1 < stages:
-                accs[c][s][...] = total
-                copy_of(c, s + 1).start()
-            else:
-                out_ref[c] = total
+                quantize(c, s + 1)
+                for copy in copies_of(c, s + 1):
+                    copy.start()
     for s in range(stages):
         for c in range(len(plans)):
-            copy_of(c, s).wait_send()
+            for copy in copies_of(c, s):
+                copy.wait_send()
 
 
 def expand_kernel(n_tiles, x_ref, meta_ref, out_ref):
@@ -212,14 +255,16 @@
             jax.ShapeDtypeStruct((chunks, rows, LANES), jnp.float32),
             jax.ShapeDtypeStruct((2 * NI * n_tiles,), jnp.int32),
         ),
-        in_specs=[vmem, hbm, smem, smem],
+        in_specs=[hbm, hbm, smem, smem],
         out_specs=(vmem, smem),
         scratch_shapes=[
-            pltpu.VMEM((k_local * LABELS, width // grain, grain, rows), jnp.bfloat16),
+            pltpu.VMEM((k_local, rows, width), jnp.bfloat16),
+            pltpu.VMEM((LABELS, k_local, width // grain, grain, rows), jnp.bfloat16),
             pltpu.SMEM((LABELS * slots,), jnp.int32),
             pltpu.SMEM((LABELS * NI * slots,), jnp.int32),
             pltpu.SMEM((LABELS,), jnp.int32),
-            pltpu.SemaphoreType.DMA((k_local, LABELS, width // grain)),
+            pltpu.SemaphoreType.DMA,
+            pltpu.SemaphoreType.DMA((LABELS, width // grain)),
         ],
         compiler_params=pltpu.CompilerParams(vmem_limit_bytes=40 * 2**20),
         name="local",
@@ -235,7 +280,11 @@
             axis = left.index((name, bit))
             left.pop(axis)
             plan.append((name, bit, axis))
-            scratch += [pltpu.VMEM((2,) * len(left) + (share, LANES), jnp.float32)] * 2
+            lead = (2,) * len(left)
+            whole = pltpu.VMEM(lead + (share, LANES), jnp.float32)
+            coded = pltpu.VMEM(lead + (share, LANES), jnp.int16)
+            scale = pltpu.VMEM(lead + (1, LANES), jnp.float32)
+            scratch += [whole, whole] if not plan[1:] else [whole, coded, coded, scale, scale]
         plans.append(plan)
     stages = amp_bits + own_bits
     summed = pl.pallas_call(
@@ -244,7 +293,7 @@
         in_specs=[vmem],
         out_specs=vmem,
         scratch_shapes=scratch
-        + [pltpu.SemaphoreType.DMA((chunks, stages)), pltpu.SemaphoreType.DMA((chunks, stages))],
+        + [pltpu.SemaphoreType.DMA((chunks, stages))] * 4,
         compiler_params=pltpu.CompilerParams(
             collective_id=0, has_side_effects=True, vmem_limit_bytes=40 * 2**20
         ),

time: 51.5 us -> 45 us (0.87)
  Pallas kernels: 46 us -> 39.5 us
    pallas_call x1, Pallas kernels: 31.5 us -> 25.2 us  [shards(): pl.pallas_call(functools.partial(scatter_kernel, plans), out_shape=jax.Sh...]
where the time goes in v2:
time: 45 us; the launch traced here: 44.8 us
  Pallas kernels  39.5 us (88%)
  local copies, waits for them, and re-layouts  5.2 us (12%)
    pallas_call x1, Pallas kernels, shards(): pl.pallas_call(functools.partial(scatter_kernel, plans), out_shape=jax.Sh...  25.2 us
    pallas_call x1, Pallas kernels, shards(): pl.pallas_call(functools.partial(local_kernel, n_tiles, slots), out_shape...  11.5 us
    unnamed x9, local copies, waits for them, and re-layouts  5.2 us
    pallas_call x1, Pallas kernels, shards(): pl.pallas_call(functools.partial(expand_kernel, n_tiles), out_shape=jax.S...  2.79 us

profile of v2, /device:TPU:0, one launch (start us, length us, event | category | flops | bytes accessed | tf_op | source)
XLA Modules:
  0.0 44.8 jit_solution(2742771060638611582)
XLA Ops:
  0.0 2.7 %copy.5.amp_hbm = bf16[4,2304,48]{2,1,0:T(8,128)(2,1)S(1)} copy(bf16[4,2304,48]{1,2,0:T(8,128)(2,1)} %param.4) | data formatting | bytes 1769472 | tf_op args[0]
  2.7 0.0 copy-start.1
  2.7 0.6 %copy-done.1 = s32[34]{0:T(128)S(1)} copy-done((s32[34]{0:T(128)S(1)}, s32[34]{0:T(128)}, u32[]{:S(2)}) %copy-start.1) | copy-done | bytes 160
  3.4 0.0 copy-start.2
  3.4 0.7 %copy-done.2 = s32[18]{0:T(128)S(1)} copy-done((s32[18]{0:T(128)S(1)}, s32[18]{0:T(128)}, u32[]{:S(2)}) %copy-start.2) | copy-done | bytes 96
  4.0 11.5 %local.1 = (f32[3,2304,128]{2,1,0:T(8,128)S(1)}, s32[72]{0:T(128)S(1)}) custom-call(bf16[4,2304,48]{2,1,0:T(8,128)(2,1)S(1)} %copy.5.amp_hbm, bf16[4,1152,2304]{2,1,0:T(8,128)(2,1)} %int_ref.1, s32[34]{0:T(128)S(1)} %copy-done.1, s32[18]{0:T(128)S(1)} %copy-done.2), custom_call_target="tpu_custom_call" | custom-call | tf_op jit(solution)/shard_map/local/pallas_call | solution.py:252
  15.5 0.0 copy-start.3
  15.5 0.6 %copy-done.3 = s32[72]{0:T(128)} copy-done((s32[72]{0:T(128)}, s32[72]{0:T(128)S(1)}, u32[]{:S(2)}) %copy-start.3) | copy-done | bytes 312
  16.1 25.2 %scatter.1.x_ref = f32[3,72,128]{2,1,0:T(8,128)S(1)} custom-call(f32[3,2,2,2,2,2,72,128]{7,6,5,4,3,2,1,0:T(8,128)S(1)} %bitcast.1), custom_call_target="tpu_custom_call" | custom-call | tf_op jit(solution)/shard_map/scatter/pallas_call | solution.py:290
  41.3 0.0 copy-start
  41.3 0.6 %copy-done = f32[3,72,128]{2,1,0:T(8,128)} copy-done((f32[3,72,128]{2,1,0:T(8,128)}, f32[3,72,128]{2,1,0:T(8,128)S(1)}, u32[]{:S(2)}) %copy-start) | copy-done | bytes 110616
  42.0 2.8 %expand.1 = bf16[72,2304]{1,0:T(8,128)(2,1)} custom-call(f32[3,72,128]{2,1,0:T(8,128)} %copy-done, s32[72]{0:T(128)} %copy-done.3), custom_call_target="tpu_custom_call" | custom-call | tf_op jit(solution)/shard_map/expand/pallas_call | solution.py:303
Async XLA Ops:
  2.7 0.7 %copy-start.1 = (s32[34]{0:T(128)S(1)}, s32[34]{0:T(128)}, u32[]{:S(2)}) copy-start(s32[34]{0:T(128)} %occ_ref.1) | copy-start | bytes 412
  3.4 0.7 %copy-start.2 = (s32[18]{0:T(128)S(1)}, s32[18]{0:T(128)}, u32[]{:S(2)}) copy-start(s32[18]{0:T(128)} %tile_ref.1) | copy-start | bytes 220
  15.5 0.6 %copy-start.3 = (s32[72]{0:T(128)}, s32[72]{0:T(128)S(1)}, u32[]{:S(2)}) copy-start(s32[72]{0:T(128)S(1)} %get-tuple-element.8.meta_ref) | copy-start | bytes 868
  41.3 0.6 %copy-start = (f32[3,72,128]{2,1,0:T(8,128)}, f32[3,72,128]{2,1,0:T(8,128)S(1)}, u32[]{:S(2)}) copy-start(f32[3,72,128]{2,1,0:T(8,128)S(1)} %scatter.1.x_ref) | copy-start | bytes 331780

commit v3 on v2

--- a/solution.py
+++ b/solution.py
@@ -21,16 +21,19 @@
     return a if b == 0 else gcd(b, a % b)
 
 
-def half_of(block, odd):
-    return jnp.where(odd, block[:, TILE:], block[:, :TILE])
-
-
-def local_kernel(n_tiles, slots, amp_hbm, int_ref, occ_ref, tile_ref, out_ref, meta_ref, amp_ref, w_ref, tile_of, row_of, count, amp_sem, sems):
-    k_local, rows, width = amp_hbm.shape
+def local_kernel(n_tiles, slots, amp_hbm, int_ref, occ_hbm, tile_hbm, out_ref, amp_ref, w_ref, occ_ref, tile_ref, tile_of, row_of, count, local_sems, sems):
+    k_local, width, rows = amp_hbm.shape
     pieces, grain = w_ref.shape[2], w_ref.shape[3]
     wide = NI * slots
     amp_index = lax.axis_index("amp")
     own_index = lax.axis_index("own")
+
+    amp_copy = pltpu.make_async_copy(amp_hbm, amp_ref, local_sems.at[0])
+    occ_copy = pltpu.make_async_copy(occ_hbm, occ_ref, local_sems.at[1])
+    tile_copy = pltpu.make_async_copy(tile_hbm, tile_ref, local_sems.at[2])
+    tile_copy.start()
+    occ_copy.start()
+    amp_copy.start()
 
     for i in range(LABELS):
         count[i] = 0
@@ -38,14 +41,12 @@
             tile_of[i * slots + s] = -1
         for q in range(wide):
             row_of[i * wide + q] = -1
+    tile_copy.wait()
     for t in range(n_tiles):
         lab = tile_ref[t]
         rank = count[lab]
         tile_of[lab * slots + rank] = t
         count[lab] = rank + 1
-
-    amp_copy = pltpu.make_async_copy(amp_hbm, amp_ref, amp_sem)
-    amp_copy.start()
 
     def copy_of(lab, j):
         at = amp_index * width + j * grain
@@ -68,13 +69,12 @@
 
     for i in range(LABELS):
         count[i] = 0
+    occ_copy.wait()
     for u in range(NI * n_tiles):
         lab = jnp.bitwise_xor(occ_ref[u // n_tiles], tile_ref[u % n_tiles])
         rank = count[lab]
         row_of[lab * wide + rank] = u
         count[lab] = rank + 1
-        meta_ref[u] = lab
-        meta_ref[NI * n_tiles + u] = rank
 
     k_lab = [occ_ref[NI + own_index * k_local + k] for k in range(k_local)]
 
@@ -87,29 +87,26 @@
             def _():
                 copy.wait()
 
+    low = lax.broadcasted_iota(jnp.int32, (width, LANES), 1) < TILE
+
     def block(lab, carry):
         tiles = [jnp.maximum(row_of[lab * wide + q], 0) for q in range(wide)]
-        a = jnp.concatenate(
-            [
-                jnp.concatenate(
-                    [amp_ref[k, pl.ds(pl.multiple_of(u * TILE, TILE), TILE), :] for k in range(k_local)], axis=1
-                )
-                for u in tiles
-            ],
-            axis=0,
-        )
-        stack = []
-        for k in range(k_local):
-            at = jnp.bitwise_xor(lab, k_lab[k])
-            halves = []
-            for u in tiles:
-                lanes = pl.ds(pl.multiple_of(u // 2 * LANES, LANES), LANES)
-                x = w_ref[at, k, :, :, lanes].reshape(pieces * grain, LANES)
-                halves.append(half_of(x, u % 2 == 1))
-            stack.append(jnp.concatenate(halves, axis=1))
-        w = jnp.concatenate(stack, axis=0)
-        s = jnp.dot(a, w, preferred_element_type=jnp.float32) + lax.dot_general(
-            w, a, (((0,), (1,)), ((), ())), preferred_element_type=jnp.float32
+        lanes = [pl.ds(pl.multiple_of(u // 2 * LANES, LANES), LANES) for u in tiles]
+
+        def gather(load):
+            turned = [pltpu.roll(load(at), (u + q) % 2 * TILE, 1) for q, (at, u) in enumerate(zip(lanes, tiles))]
+            return jnp.concatenate([jnp.where(low, *turned[q : q + 2]) for q in range(0, wide, 2)], axis=1)
+
+        a = [gather(lambda at: amp_ref[k, :, at]) for k in range(k_local)]
+        w = [
+            gather(lambda at: w_ref[jnp.bitwise_xor(lab, k_lab[k]), k, :, :, at].reshape(width, LANES))
+            for k in range(k_local)
+        ]
+        s = lax.dot_general(
+            jnp.concatenate(a + w, axis=0),
+            jnp.concatenate(w + a, axis=0),
+            (((0,), (0,)), ((), ())),
+            preferred_element_type=jnp.float32,
         )
         for q in range(wide):
             u = row_of[lab * wide + q]
@@ -142,7 +139,7 @@
     return {name: lax.axis_index(name) + (1 - 2 * bit_of(name, bit)) * 2**bit}
 
 
-def scatter_kernel(plans, x_ref, out_ref, *scratch):
+def scatter_kernel(plans, x_ref, occ_ref, tile_ref, out_ref, *scratch):
     stages = len(plans[0])
     bufs, at = [], 0
     for c in range(len(plans)):
@@ -151,7 +148,7 @@
             take = 2 if s == 0 else 5
             bufs[c].append(scratch[at : at + take])
             at += take
-    send_sems, recv_sems, scale_send_sems, scale_recv_sems = scratch[at:]
+    fin_ref, lab_ref, rank_ref, send_sems, recv_sems, scale_send_sems, scale_recv_sems = scratch[at:]
 
     barrier = pltpu.get_barrier_semaphore()
     for name, bit, _ in plans[0]:
@@ -196,6 +193,14 @@
     for c in range(len(plans)):
         for copy in copies_of(c, 0):
             copy.start()
+    n_tiles = tile_ref.shape[0]
+    labs = [jnp.bitwise_xor(occ_ref[u // n_tiles], tile_ref[u % n_tiles]) for u in range(NI * n_tiles)]
+    for u, lab in enumerate(labs):
+        lab_ref[u] = lab
+        rank = jnp.int32(0)
+        for other in labs[:u]:
+            rank = rank + jnp.where(other == lab, 1, 0)
+        rank_ref[u] = rank
     for s in range(stages):
         for c in range(len(plans)):
             name, bit, axis = plans[c][s]
@@ -212,7 +217,7 @@
                 if s + 1 < stages:
                     bufs[c][s][0][index] = total
                 else:
-                    out_ref[c] = total
+                    fin_ref[c] = total
             if s + 1 < stages:
                 quantize(c, s + 1)
                 for copy in copies_of(c, s + 1):
@@ -221,23 +226,22 @@
         for c in range(len(plans)):
             for copy in copies_of(c, s):
                 copy.wait_send()
-
-
-def expand_kernel(n_tiles, x_ref, meta_ref, out_ref):
-    chunks, share, _ = x_ref.shape
-    count = NI * n_tiles
-    base = (lax.axis_index("amp") * lax.axis_size("own") + lax.axis_index("own")) * share
+    base = (lax.axis_index("amp") * lax.axis_size("own") + lax.axis_index("own")) * fin_ref.shape[1]
+    expand(base, fin_ref, lab_ref, rank_ref, out_ref)
+
+
+def expand(base, x_ref, lab_ref, rank_ref, out_ref):
+    share = x_ref.shape[1]
+    count = lab_ref.shape[0]
     first = base // TILE
     row = base + lax.broadcasted_iota(jnp.int32, (share, LANES), 0)
-    lane = lax.broadcasted_iota(jnp.int32, (share, LANES), 1)
-    row_lab = jnp.where(row < (first + 1) * TILE, meta_ref[first], meta_ref[jnp.minimum(first + 1, count - 1)])
-    for pair in range(count // 2):
-        labs = [meta_ref[2 * pair + h] for h in range(2)]
-        ranks = [meta_ref[count + 2 * pair + h] for h in range(2)]
-        halves = [half_of(x_ref[rank // 2], rank % 2 == 1) for rank in ranks]
-        col_lab = jnp.where(lane < TILE, labs[0], labs[1])
-        dense = jnp.where(row_lab == col_lab, jnp.concatenate(halves, axis=1), 0.0)
-        out_ref[:, pair * LANES : (pair + 1) * LANES] = dense.astype(out_ref.dtype)
+    low = lax.broadcasted_iota(jnp.int32, (share, LANES), 1) < TILE
+    row_lab = jnp.where(row < (first + 1) * TILE, lab_ref[first], lab_ref[jnp.minimum(first + 1, count - 1)])
+    for u in range(0, count, 2):
+        ranks = [rank_ref[u + h] for h in range(2)]
+        turned = [pltpu.roll(x_ref[jnp.minimum(rank // 2, x_ref.shape[0] - 1)], (rank + h) % 2 * TILE, 1) for h, rank in enumerate(ranks)]
+        match = row_lab == jnp.where(low, lab_ref[u], lab_ref[u + 1])
+        out_ref[:, u * TILE : (u + 2) * TILE] = jnp.where(match, jnp.where(low, *turned), 0.0).astype(out_ref.dtype)
 
 
 def shards(amplitudes, integrals, occ_irrep, tile_irrep):
@@ -248,27 +252,26 @@
     slots = width * n_amp // TILE
     grain = gcd(width, TILE)
     chunks = NI * slots * TILE // LANES
-    vmem, smem, hbm = (pl.BlockSpec(memory_space=m) for m in (pltpu.VMEM, pltpu.SMEM, pl.ANY))
-    packed, meta = pl.pallas_call(
+    vmem, smem, hbm = (pl.BlockSpec(memory_space=m) for m in (pltpu.VMEM, pltpu.SMEM, pltpu.HBM))
+    packed = pl.pallas_call(
         functools.partial(local_kernel, n_tiles, slots),
-        out_shape=(
-            jax.ShapeDtypeStruct((chunks, rows, LANES), jnp.float32),
-            jax.ShapeDtypeStruct((2 * NI * n_tiles,), jnp.int32),
-        ),
-        in_specs=[hbm, hbm, smem, smem],
-        out_specs=(vmem, smem),
+        out_shape=jax.ShapeDtypeStruct((chunks, rows, LANES), jnp.float32),
+        in_specs=[hbm] * 4,
+        out_specs=vmem,
         scratch_shapes=[
-            pltpu.VMEM((k_local, rows, width), jnp.bfloat16),
+            pltpu.VMEM((k_local, width, rows), jnp.bfloat16),
             pltpu.VMEM((LABELS, k_local, width // grain, grain, rows), jnp.bfloat16),
+            pltpu.SMEM(occ_irrep.shape, jnp.int32),
+            pltpu.SMEM(tile_irrep.shape, jnp.int32),
             pltpu.SMEM((LABELS * slots,), jnp.int32),
             pltpu.SMEM((LABELS * NI * slots,), jnp.int32),
             pltpu.SMEM((LABELS,), jnp.int32),
-            pltpu.SemaphoreType.DMA,
+            pltpu.SemaphoreType.DMA((3,)),
             pltpu.SemaphoreType.DMA((LABELS, width // grain)),
         ],
         compiler_params=pltpu.CompilerParams(vmem_limit_bytes=40 * 2**20),
         name="local",
-    )(amplitudes, integrals, occ_irrep, tile_irrep)
+    )(jnp.swapaxes(amplitudes, 1, 2), integrals, occ_irrep, tile_irrep)
 
     amp_bits, own_bits = n_amp.bit_length() - 1, n_own.bit_length() - 1
     share = rows // (n_amp * n_own)
@@ -287,26 +290,20 @@
             scratch += [whole, whole] if not plan[1:] else [whole, coded, coded, scale, scale]
         plans.append(plan)
     stages = amp_bits + own_bits
-    summed = pl.pallas_call(
+    return pl.pallas_call(
         functools.partial(scatter_kernel, plans),
-        out_shape=jax.ShapeDtypeStruct((chunks, share, LANES), jnp.float32),
-        in_specs=[vmem],
+        out_shape=jax.ShapeDtypeStruct((share, rows), jnp.bfloat16),
+        in_specs=[vmem, smem, smem],
         out_specs=vmem,
         scratch_shapes=scratch
+        + [pltpu.VMEM((chunks, share, LANES), jnp.float32)]
+        + [pltpu.SMEM((NI * n_tiles,), jnp.int32)] * 2
         + [pltpu.SemaphoreType.DMA((chunks, stages))] * 4,
         compiler_params=pltpu.CompilerParams(
             collective_id=0, has_side_effects=True, vmem_limit_bytes=40 * 2**20
         ),
         name="scatter",
-    )(packed.reshape((chunks,) + (2,) * stages + (share, LANES)))
-
-    return pl.pallas_call(
-        functools.partial(expand_kernel, n_tiles),
-        out_shape=jax.ShapeDtypeStruct((share, rows), jnp.bfloat16),
-        in_specs=[vmem, smem],
-        out_specs=vmem,
-        name="expand",
-    )(summed, meta)
+    )(packed.reshape((chunks,) + (2,) * stages + (share, LANES)), occ_irrep, tile_irrep)
 
 
 def solution(mesh):

time: 45 us -> 39 us (0.87)
  Pallas kernels: 39.5 us -> 35.6 us
  local copies, waits for them, and re-layouts: 5.2 us -> 3.2 us
    pallas_call x1 -> x0, Pallas kernels: 2.79 us -> none  [shards(): pl.pallas_call(functools.partial(expand_kernel, n_tiles), out_shape=jax.S...]
    pallas_call x1, Pallas kernels: 11.5 us -> 9.47 us  [shards(): pl.pallas_call(functools.partial(local_kernel, n_tiles, slots), out_shape...]
    unnamed x9 -> x7, local copies, waits for them, and re-layouts: 5.2 us -> 3.2 us
    pallas_call x1, Pallas kernels: 25.2 us -> 26.2 us  [shards(): pl.pallas_call(functools.partial(scatter_kernel, plans), out_shape=jax.Sh...]
where the time goes in v3:
time: 39 us; the launch traced here: 38.8 us
  Pallas kernels  35.6 us (91%)
  local copies, waits for them, and re-layouts  3.2 us (8%)
    pallas_call x1, Pallas kernels, shards(): pl.pallas_call(functools.partial(scatter_kernel, plans), out_shape=jax.Sh...  26.2 us
    pallas_call x1, Pallas kernels, shards(): pl.pallas_call(functools.partial(local_kernel, n_tiles, slots), out_shape...  9.47 us
    unnamed x7, local copies, waits for them, and re-layouts  3.2 us

profile of v3, /device:TPU:0, one launch (start us, length us, event | category | flops | bytes accessed | tf_op | source)
XLA Modules:
  0.0 38.8 jit_solution(15578811875031671999)
XLA Ops:
  0.0 0.0 copy-start
  0.0 1.2 %copy-done = bf16[4,2304,48]{1,2,0:T(8,128)(2,1)S(1)} copy-done((bf16[4,2304,48]{1,2,0:T(8,128)(2,1)S(1)}, bf16[4,2304,48]{1,2,0:T(8,128)(2,1)}, u32[]{:S(2)}) %copy-start) | copy-done | bytes 884760
  1.2 0.0 copy-start.1
  1.2 0.7 %copy-done.1 = s32[34]{0:T(128)S(1)} copy-done((s32[34]{0:T(128)S(1)}, s32[34]{0:T(128)}, u32[]{:S(2)}) %copy-start.1) | copy-done | bytes 160
  1.8 0.0 copy-start.2
  1.8 0.7 %copy-done.2 = s32[18]{0:T(128)S(1)} copy-done((s32[18]{0:T(128)S(1)}, s32[18]{0:T(128)}, u32[]{:S(2)}) %copy-start.2) | copy-done | bytes 96
  2.5 9.5 %local.1 = f32[3,2304,128]{2,1,0:T(8,128)S(1)} custom-call(bf16[4,48,2304]{2,1,0:T(8,128)(2,1)S(1)} %bitcast.3, bf16[4,1152,2304]{2,1,0:T(8,128)(2,1)} %int_ref.1, s32[34]{0:T(128)S(1)} %copy-done.1, s32[18]{0:T(128)S(1)} %copy-done.2), custom_call_target="tpu_custom_call" | custom-call | tf_op jit(solution)/shard_map/local/pallas_call | solution.py:256
  12.0 26.2 %scatter.1 = bf16[72,2304]{1,0:T(8,128)(2,1)S(1)} custom-call(f32[3,2,2,2,2,2,72,128]{7,6,5,4,3,2,1,0:T(8,128)S(1)} %bitcast.2, s32[34]{0:T(128)S(1)} %copy-done.1, s32[18]{0:T(128)S(1)} %copy-done.2), custom_call_target="tpu_custom_call" | custom-call | tf_op jit(solution)/shard_map/scatter/pallas_call | solution.py:293
  38.1 0.7 %copy.6 = bf16[72,2304]{1,0:T(8,128)(2,1)} copy(bf16[72,2304]{1,0:T(8,128)(2,1)S(1)} %scatter.1) | data formatting | bytes 663552
Async XLA Ops:
  0.0 1.2 %copy-start = (bf16[4,2304,48]{1,2,0:T(8,128)(2,1)S(1)}, bf16[4,2304,48]{1,2,0:T(8,128)(2,1)}, u32[]{:S(2)}) copy-start(bf16[4,2304,48]{1,2,0:T(8,128)(2,1)} %param.4) | copy-start | bytes 2654212
  1.2 0.7 %copy-start.1 = (s32[34]{0:T(128)S(1)}, s32[34]{0:T(128)}, u32[]{:S(2)}) copy-start(s32[34]{0:T(128)} %occ_ref.1) | copy-start | bytes 412
  1.8 0.7 %copy-start.2 = (s32[18]{0:T(128)S(1)}, s32[18]{0:T(128)}, u32[]{:S(2)}) copy-start(s32[18]{0:T(128)} %tile_ref.1) | copy-start | bytes 220

commit v4 on v3

--- a/solution.py
+++ b/solution.py
@@ -180,12 +180,20 @@
     def blocks(count):
         return itertools.product(range(2), repeat=count)
 
+    def total_of(c, s, index):
+        name, bit, axis = plans[c][s]
+        kept = index[:axis] + (bit_of(name, bit),) + index[axis:]
+        if s == 0:
+            return x_ref[(c,) + kept] + bufs[c][s][1][index]
+        _, _, q_recv, _, scale_recv = bufs[c][s]
+        return bufs[c][s - 1][0][kept] + q_recv[index].astype(jnp.int32).astype(jnp.float32) * scale_recv[index]
+
     def quantize(c, s):
         name, bit, axis = plans[c][s]
         _, q_send, _, scale_send, _ = bufs[c][s]
         away = 1 - bit_of(name, bit)
         for index in blocks(stages - 1 - s):
-            x = bufs[c][s - 1][0][index[:axis] + (away,) + index[axis:]]
+            x = total_of(c, s - 1, index[:axis] + (away,) + index[axis:])
             most = jnp.maximum(jnp.max(jnp.abs(x), axis=0, keepdims=True), LEAST)
             q_send[index] = jnp.round(x * (LEVELS / most)).astype(jnp.int32).astype(jnp.int16)
             scale_send[index] = most * (1.0 / LEVELS)
@@ -203,25 +211,18 @@
         rank_ref[u] = rank
     for s in range(stages):
         for c in range(len(plans)):
-            name, bit, axis = plans[c][s]
-            keep = bit_of(name, bit)
             for copy in copies_of(c, s):
                 copy.wait_recv()
-            for index in blocks(stages - 1 - s):
-                kept = index[:axis] + (keep,) + index[axis:]
-                if s == 0:
-                    total = x_ref[(c,) + kept] + bufs[c][s][1][index]
-                else:
-                    _, _, q_recv, _, scale_recv = bufs[c][s]
-                    total = bufs[c][s - 1][0][kept] + q_recv[index].astype(jnp.int32).astype(jnp.float32) * scale_recv[index]
-                if s + 1 < stages:
-                    bufs[c][s][0][index] = total
-                else:
-                    fin_ref[c] = total
-            if s + 1 < stages:
-                quantize(c, s + 1)
-                for copy in copies_of(c, s + 1):
-                    copy.start()
+            if s + 1 == stages:
+                fin_ref[c] = total_of(c, s, ())
+                continue
+            quantize(c, s + 1)
+            for copy in copies_of(c, s + 1):
+                copy.start()
+            name, bit, axis = plans[c][s + 1]
+            for index in blocks(stages - 2 - s):
+                kept = index[:axis] + (bit_of(name, bit),) + index[axis:]
+                bufs[c][s][0][kept] = total_of(c, s, kept)
     for s in range(stages):
         for c in range(len(plans)):
             for copy in copies_of(c, s):

time: 39 us -> 38.8 us (level)
  no operation moved by 1% of the time
where the time goes in v4:
time: 38.8 us; the launch traced here: 38.6 us
  Pallas kernels  35.4 us (91%)
  local copies, waits for them, and re-layouts  3.2 us (8%)
    pallas_call x1, Pallas kernels, shards(): pl.pallas_call(functools.partial(scatter_kernel, plans), out_shape=jax.Sh...  25.9 us
    pallas_call x1, Pallas kernels, shards(): pl.pallas_call(functools.partial(local_kernel, n_tiles, slots), out_shape...  9.48 us
    unnamed x7, local copies, waits for them, and re-layouts  3.2 us

profile of v4, /device:TPU:0, one launch (start us, length us, event | category | flops | bytes accessed | tf_op | source)
XLA Modules:
  0.0 38.6 jit_solution(14873059880133681918)
XLA Ops:
  0.0 0.0 copy-start
  0.0 1.2 %copy-done = bf16[4,2304,48]{1,2,0:T(8,128)(2,1)S(1)} copy-done((bf16[4,2304,48]{1,2,0:T(8,128)(2,1)S(1)}, bf16[4,2304,48]{1,2,0:T(8,128)(2,1)}, u32[]{:S(2)}) %copy-start) | copy-done | bytes 884760
  1.2 0.0 copy-start.1
  1.2 0.7 %copy-done.1 = s32[34]{0:T(128)S(1)} copy-done((s32[34]{0:T(128)S(1)}, s32[34]{0:T(128)}, u32[]{:S(2)}) %copy-start.1) | copy-done | bytes 160
  1.8 0.0 copy-start.2
  1.8 0.7 %copy-done.2 = s32[18]{0:T(128)S(1)} copy-done((s32[18]{0:T(128)S(1)}, s32[18]{0:T(128)}, u32[]{:S(2)}) %copy-start.2) | copy-done | bytes 96
  2.5 9.5 %local.1 = f32[3,2304,128]{2,1,0:T(8,128)S(1)} custom-call(bf16[4,48,2304]{2,1,0:T(8,128)(2,1)S(1)} %bitcast.3, bf16[4,1152,2304]{2,1,0:T(8,128)(2,1)} %int_ref.1, s32[34]{0:T(128)S(1)} %copy-done.1, s32[18]{0:T(128)S(1)} %copy-done.2), custom_call_target="tpu_custom_call" | custom-call | tf_op jit(solution)/shard_map/local/pallas_call | solution.py:257
  12.0 25.9 %scatter.1 = bf16[72,2304]{1,0:T(8,128)(2,1)S(1)} custom-call(f32[3,2,2,2,2,2,72,128]{7,6,5,4,3,2,1,0:T(8,128)S(1)} %bitcast.2, s32[34]{0:T(128)S(1)} %copy-done.1, s32[18]{0:T(128)S(1)} %copy-done.2), custom_call_target="tpu_custom_call" | custom-call | tf_op jit(solution)/shard_map/scatter/pallas_call | solution.py:294
  37.9 0.7 %copy.6 = bf16[72,2304]{1,0:T(8,128)(2,1)} copy(bf16[72,2304]{1,0:T(8,128)(2,1)S(1)} %scatter.1) | data formatting | bytes 663552
Async XLA Ops:
  0.0 1.2 %copy-start = (bf16[4,2304,48]{1,2,0:T(8,128)(2,1)S(1)}, bf16[4,2304,48]{1,2,0:T(8,128)(2,1)}, u32[]{:S(2)}) copy-start(bf16[4,2304,48]{1,2,0:T(8,128)(2,1)} %param.4) | copy-start | bytes 2654212
  1.2 0.7 %copy-start.1 = (s32[34]{0:T(128)S(1)}, s32[34]{0:T(128)}, u32[]{:S(2)}) copy-start(s32[34]{0:T(128)} %occ_ref.1) | copy-start | bytes 412
  1.8 0.7 %copy-start.2 = (s32[18]{0:T(128)S(1)}, s32[18]{0:T(128)}, u32[]{:S(2)}) copy-start(s32[18]{0:T(128)} %tile_ref.1) | copy-start | bytes 220

commit v5 on v4

--- a/solution.py
+++ b/solution.py
@@ -21,19 +21,17 @@
     return a if b == 0 else gcd(b, a % b)
 
 
-def local_kernel(n_tiles, slots, amp_hbm, int_ref, occ_hbm, tile_hbm, out_ref, amp_ref, w_ref, occ_ref, tile_ref, tile_of, row_of, count, local_sems, sems):
-    k_local, width, rows = amp_hbm.shape
+def local_kernel(n_tiles, slots, amp_ref, int_ref, occ_hbm, tile_hbm, out_ref, w_ref, occ_ref, tile_ref, tile_of, row_of, count, local_sems, sems):
+    k_local, width, rows = amp_ref.shape
     pieces, grain = w_ref.shape[2], w_ref.shape[3]
     wide = NI * slots
     amp_index = lax.axis_index("amp")
     own_index = lax.axis_index("own")
 
-    amp_copy = pltpu.make_async_copy(amp_hbm, amp_ref, local_sems.at[0])
     occ_copy = pltpu.make_async_copy(occ_hbm, occ_ref, local_sems.at[1])
     tile_copy = pltpu.make_async_copy(tile_hbm, tile_ref, local_sems.at[2])
     tile_copy.start()
     occ_copy.start()
-    amp_copy.start()
 
     for i in range(LABELS):
         count[i] = 0
@@ -78,7 +76,6 @@
 
     k_lab = [occ_ref[NI + own_index * k_local + k] for k in range(k_local)]
 
-    amp_copy.wait()
     for lab in range(LABELS):
         for j in range(pieces):
             t, copy = copy_of(lab, j)
@@ -257,10 +254,9 @@
     packed = pl.pallas_call(
         functools.partial(local_kernel, n_tiles, slots),
         out_shape=jax.ShapeDtypeStruct((chunks, rows, LANES), jnp.float32),
-        in_specs=[hbm] * 4,
+        in_specs=[vmem] + [hbm] * 3,
         out_specs=vmem,
         scratch_shapes=[
-            pltpu.VMEM((k_local, width, rows), jnp.bfloat16),
             pltpu.VMEM((LABELS, k_local, width // grain, grain, rows), jnp.bfloat16),
             pltpu.SMEM(occ_irrep.shape, jnp.int32),
             pltpu.SMEM(tile_irrep.shape, jnp.int32),

time: 38.8 us -> 38.8 us (level)
  no operation moved by 1% of the time
where the time goes in v5:
time: 38.8 us; the launch traced here: 38.6 us
  Pallas kernels  35.4 us (91%)
  local copies, waits for them, and re-layouts  3.2 us (8%)
    pallas_call x1, Pallas kernels, shards(): pl.pallas_call(functools.partial(scatter_kernel, plans), out_shape=jax.Sh...  25.9 us
    pallas_call x1, Pallas kernels, shards(): pl.pallas_call(functools.partial(local_kernel, n_tiles, slots), out_shape...  9.47 us
    unnamed x7, local copies, waits for them, and re-layouts  3.2 us

profile of v5, /device:TPU:0, one launch (start us, length us, event | category | flops | bytes accessed | tf_op | source)
XLA Modules:
  0.0 38.6 jit_solution(12281044801464114925)
XLA Ops:
  0.0 0.0 copy-start
  0.0 1.2 %copy-done = bf16[4,2304,48]{1,2,0:T(8,128)(2,1)S(1)} copy-done((bf16[4,2304,48]{1,2,0:T(8,128)(2,1)S(1)}, bf16[4,2304,48]{1,2,0:T(8,128)(2,1)}, u32[]{:S(2)}) %copy-start) | copy-done | bytes 884760
  1.2 0.0 copy-start.1
  1.2 0.7 %copy-done.1 = s32[34]{0:T(128)S(1)} copy-done((s32[34]{0:T(128)S(1)}, s32[34]{0:T(128)}, u32[]{:S(2)}) %copy-start.1) | copy-done | bytes 160
  1.8 0.0 copy-start.2
  1.8 0.7 %copy-done.2 = s32[18]{0:T(128)S(1)} copy-done((s32[18]{0:T(128)S(1)}, s32[18]{0:T(128)}, u32[]{:S(2)}) %copy-start.2) | copy-done | bytes 96
  2.5 9.5 %local.1 = f32[3,2304,128]{2,1,0:T(8,128)S(1)} custom-call(bf16[4,48,2304]{2,1,0:T(8,128)(2,1)S(1)} %bitcast.3, bf16[4,1152,2304]{2,1,0:T(8,128)(2,1)} %int_ref.1, s32[34]{0:T(128)S(1)} %copy-done.1, s32[18]{0:T(128)S(1)} %copy-done.2), custom_call_target="tpu_custom_call" | custom-call | tf_op jit(solution)/shard_map/local/pallas_call | solution.py:254
  12.0 25.9 %scatter.1 = bf16[72,2304]{1,0:T(8,128)(2,1)S(1)} custom-call(f32[3,2,2,2,2,2,72,128]{7,6,5,4,3,2,1,0:T(8,128)S(1)} %bitcast.2, s32[34]{0:T(128)S(1)} %copy-done.1, s32[18]{0:T(128)S(1)} %copy-done.2), custom_call_target="tpu_custom_call" | custom-call | tf_op jit(solution)/shard_map/scatter/pallas_call | solution.py:290
  37.9 0.7 %copy.6 = bf16[72,2304]{1,0:T(8,128)(2,1)} copy(bf16[72,2304]{1,0:T(8,128)(2,1)S(1)} %scatter.1) | data formatting | bytes 663552
Async XLA Ops:
  0.0 1.2 %copy-start = (bf16[4,2304,48]{1,2,0:T(8,128)(2,1)S(1)}, bf16[4,2304,48]{1,2,0:T(8,128)(2,1)}, u32[]{:S(2)}) copy-start(bf16[4,2304,48]{1,2,0:T(8,128)(2,1)} %param.4) | copy-start | bytes 2654212
  1.2 0.7 %copy-start.1 = (s32[34]{0:T(128)S(1)}, s32[34]{0:T(128)}, u32[]{:S(2)}) copy-start(s32[34]{0:T(128)} %occ_ref.1) | copy-start | bytes 412
  1.8 0.7 %copy-start.2 = (s32[18]{0:T(128)S(1)}, s32[18]{0:T(128)}, u32[]{:S(2)}) copy-start(s32[18]{0:T(128)} %tile_ref.1) | copy-start | bytes 220
